TPU v7x, 128 devices: a whole 4x4x4 slice. The times are simulated.
128 devices in a mesh: seq: 8 (over y, x_hi), hid: 16 (over z, x_lo, core).
Axes of the slice: x: 4 (x_hi: 2, x_lo: 2; x = x_hi * 2 + x_lo), y: 4, z: 4, core: 2. Of those that a mesh axis runs over, the one named last changes fastest.
Arguments:
- tokens: bfloat16 [5120, 5120], P('seq', 'hid'), may hold values from -18 to 18
- clip_id: int32 [5120], P('seq'), may hold values from 0 to 7, never falling along the last dimension, each value on 1 to 3200 neighbouring positions
- clip_step: int32 [8], replicated, may hold values from 0 to 31
- mod_table: float32 [32, 6, 5120], replicated, may hold values from -3 to 3
- w_query: bfloat16 [5120, 4096], P(None, 'hid'), may hold values from -3 to 3
- w_key: bfloat16 [5120, 4096], P(None, 'hid'), may hold values from -3 to 3
- w_value: bfloat16 [5120, 4096], P(None, 'hid'), may hold values from -0.078125 to 0.078125
- q_gain: float32 [4096], P('hid'), may hold values from 0.4 to 6
- k_gain: float32 [4096], P('hid'), may hold values from 0.4 to 6
- w_out: bfloat16 [4096, 5120], P('hid'), may hold values from -0.125 to 0.125
- w_up: bfloat16 [5120, 8192], P(None, 'hid'), may hold values from -0.078125 to 0.078125
- w_down: bfloat16 [8192, 5120], P('hid'), may hold values from -0.09375 to 0.09375
Outputs:
- block_out: bfloat16 [5120, 5120], P('seq', 'hid')
Inputs may be any that keep to these rules, and one draw needn't show every extreme that they name: `clip_id`: clip numbers never fall along the tokens; every clip 0 to 7 holds 1 to 3200 tokens, and one holds exactly 3200.
All inputs are finite; a program needn't handle non-finite values.
Results may differ from a plain program's by a relative error of at most 0.018.
Values may be sent and summed in bfloat16 or wider, within the bound.
A program may use at most 128 MiB of HBM per device.

v0:
```python
import functools
import jax
import jax.numpy as jnp
from jax import lax
from jax.experimental import pallas as pl
from jax.experimental.pallas import tpu as pltpu
from jax.sharding import PartitionSpec as P

MESH = pl.DeviceIdType.MESH
EPS = 1e-06
HEAD_DIM = 128
SCORE_SCALE = HEAD_DIM ** (-0.5) * 1.4426950408889634
FAR = -1e30
F32 = jnp.float32
BF16 = jnp.bfloat16
ANYSPEC = pl.BlockSpec(memory_space=pl.ANY)
VSPEC = pl.BlockSpec(memory_space=pltpu.VMEM)

OWN, XP, ZM, ZP, ZMX, ZPX, Z2, Z2X = range(8)
OFFSETS = ((0, 0), (0, 1), (3, 0), (1, 0), (3, 1), (1, 1), (2, 0), (2, 1))
BACK = (OWN, XP, ZP, ZM, ZPX, ZMX, Z2, Z2X)
Y_STEPS = (0, 3, 1, 2)
Y_BACK = (0, 2, 1, 3)
A, B = 0, 1


def hid_place():
    h = lax.axis_index("hid")
    return h // 4, lax.rem(h // 2, 2), lax.rem(h, 2)


def chip_of(role):
    z, x, _ = hid_place()
    dz, dx = OFFSETS[role]
    return lax.rem(z + dz, 4) * 2 + lax.rem(x + dx, 2)


def hid_device(role, flip):
    core = hid_place()[2]
    core = 1 - core if flip else core
    return {"hid": chip_of(role) * 2 + core}


def seq_device(y_role, flip):
    s = lax.axis_index("seq")
    y, x = s // 2, lax.rem(s, 2)
    x = 1 - x if flip else x
    return {"seq": lax.rem(y + Y_STEPS[y_role], 4) * 2 + x}


def pieces(values, count):
    parts = []
    for i in range(count - 1):
        piece = values.astype(BF16).astype(F32)
        parts.append(piece)
        values = values - piece
    return jnp.concatenate(parts + [values], axis=0).astype(BF16)


def rows_to_columns(rows, width):
    n = rows.shape[0]
    parts = pieces(rows, 3)
    pick = (
        lax.broadcasted_iota(jnp.int32, (3 * n, n * width), 1) // width
        == lax.rem(lax.broadcasted_iota(jnp.int32, (3 * n, n * width), 0), n)
    ).astype(F32).astype(BF16)
    return lax.dot_general(parts, pick, (((0,), (0,)), ((), ())), preferred_element_type=F32)


def identity(size):
    rows = lax.broadcasted_iota(jnp.int32, (size, size), 0)
    return (rows == lax.broadcasted_iota(jnp.int32, (size, size), 1)).astype(F32).astype(BF16)


def lane_sums(values):
    ones = jnp.ones((8, values.shape[1]), BF16)
    dims = (((1,), (1,)), ((), ()))
    if values.dtype == BF16:
        return lax.dot_general(ones, values, dims, preferred_element_type=F32)[0:1]
    top = values.astype(BF16)
    rest = (values - top.astype(F32)).astype(BF16)
    both = lax.dot_general(ones, top, dims, preferred_element_type=F32)
    return (both + lax.dot_general(ones, rest, dims, preferred_element_type=F32))[0:1]


def greet(hid_all, hid_near, seq):
    barrier = pltpu.get_barrier_semaphore()
    peers = [hid_device(OWN, True)]
    if hid_all:
        peers += [hid_device(r, f) for r in range(1, 8) for f in (False, True)]
    elif hid_near:
        peers += [hid_device(r, False) for r in range(1, 8)]
    if seq:
        peers += [seq_device(y, f) for y in range(4) for f in (False, True) if (y, f) != (0, False)]
    for peer in peers:
        pl.semaphore_signal(barrier, inc=1, device_id=peer, device_id_type=MESH)
    pl.semaphore_wait(barrier, len(peers))


def remote(src, dst, send_sem, recv_sem, device):
    cp = pltpu.make_async_remote_copy(src, dst, send_sem, recv_sem, device_id=device, device_id_type=MESH)
    cp.start()
    return cp


def clip_one_hot(clip_row, width, period):
    ones = jnp.ones((1, width), BF16)
    cols = lax.dot_general(clip_row.astype(BF16), ones, (((0,), (0,)), ((), ())), preferred_element_type=F32)
    lane = lax.rem(lax.broadcasted_iota(jnp.int32, cols.shape, 1), period).astype(F32)
    return cols == lane


def load_columns_of_rows(w_refs, wbuf, wsem, widths):
    full = wbuf.shape[1]
    copies = {}
    for role in (OWN, ZM, ZP, XP, Z2, ZMX, ZPX, Z2X):
        at = 0
        for i, w_ref in enumerate(w_refs):
            cp = pltpu.make_async_copy(
                w_ref.at[pl.ds(chip_of(role) * full, full)], wbuf.at[role, :, pl.ds(at, widths[i])], wsem.at[role, i]
            )
            cp.start()
            copies[role, i] = cp
            at += widths[i]
    return copies


SCATTER_ORDER = (Z2X, ZPX, ZMX, Z2, ZP, ZM, XP, OWN)


def load_blocks_of_columns(w_ref, wbuf, wsem):
    full = wbuf.shape[2]
    copies = {}
    for role in SCATTER_ORDER:
        cp = pltpu.make_async_copy(
            w_ref.at[:, pl.ds(pl.multiple_of(chip_of(role) * full, 128), full)], wbuf.at[role], wsem.at[role]
        )
        cp.start()
        copies[role] = cp
    return copies


def pair_rows(x_ref, raw, pair, psem):
    half, full = raw.shape[1], raw.shape[2]
    part = full // 2
    core = hid_place()[2]
    swap = remote(
        x_ref.at[pl.ds((1 - core) * half, half)], pair, psem.at[0], psem.at[1], hid_device(OWN, True)
    )

    def place(shift):
        rows = lax.broadcasted_iota(jnp.int32, (part, full), 0)
        cols = lax.broadcasted_iota(jnp.int32, (part, full), 1)
        return (cols == rows + shift).astype(F32).astype(BF16)

    mine = jnp.dot(x_ref[pl.ds(core * half, half)], place(core * part), preferred_element_type=F32)
    swap.wait_recv()
    block = mine + jnp.dot(pair[...], place((1 - core) * part), preferred_element_type=F32)
    raw[OWN] = block.astype(BF16)
    swap.wait_send()


def gather_phase(hot_ref, mod_ref, scale_at, w_copies, n_weights, width,
                 raw, nrm, stat, norm, wbuf, acc, ssend, srecv, rsend, rrecv, dsend, drecv, meanwhile=None, free=None):
    half, full = raw.shape[1], raw.shape[2]
    quarter = half // 2
    core = hid_place()[2]
    sends = {}

    def send_raw(slot, which, to_role, to_slot):
        rows = pl.ds(which * quarter, quarter)
        sends[to_slot, which] = remote(
            raw.at[slot, rows], raw.at[to_slot, rows], rsend.at[to_slot, which], rrecv.at[to_slot, which],
            hid_device(to_role, False),
        )

    def await_raw(slot, which):
        sends[slot, which].wait_recv()

    send_raw(OWN, A, ZP, ZM)
    send_raw(OWN, B, ZM, ZP)
    send_raw(OWN, A, XP, XP)
    block = raw[OWN].astype(F32)
    stat[OWN, 0:1] = lane_sums(raw[OWN])
    stat[OWN, 1:2] = lane_sums(block * block)
    stat_copies = [
        remote(stat.at[OWN], stat.at[BACK[r]], ssend.at[r], srecv.at[BACK[r]], hid_device(r, False))
        for r in range(1, 8)
    ]
    send_raw(OWN, B, ZP, ZM)
    send_raw(OWN, A, ZM, ZP)
    send_raw(OWN, B, XP, XP)
    d_copies = {}
    hot = [hot_ref[pl.ds(pl.multiple_of(core * half + i * quarter, quarter), quarter)] for i in range(2)]
    for cp in stat_copies:
        cp.wait_recv()
    totals = stat[0]
    for r in range(1, 8):
        totals = totals + stat[r]
    moments = rows_to_columns(totals * (1.0 / (full * 8)), 128)
    norm[0] = moments[:, 0:128]
    norm[1] = lax.rsqrt(moments[:, 128:256] - moments[:, 0:128] * moments[:, 0:128] + EPS)

    def normalize(role, which):
        col = chip_of(role) * full
        rows = pl.ds(which * quarter, quarter)

        def lane_tile(n, carry):
            here = pl.ds(pl.multiple_of(n * 128, 128), 128)
            there = pl.ds(pl.multiple_of(col + n * 128, 128), 128)
            scale = jnp.dot(hot[which], pieces(mod_ref[scale_at, :, there], 3), preferred_element_type=F32)
            shift = jnp.dot(hot[which], pieces(mod_ref[scale_at - 1, :, there], 3), preferred_element_type=F32)
            values = (raw[role, rows, here].astype(F32) - norm[0, rows]) * norm[1, rows]
            nrm[core, role, rows, here] = (values * (1.0 + scale) + shift).astype(BF16)
            return carry

        lax.fori_loop(0, full // 128, lane_tile, 0)
        d_copies[role, which] = remote(
            nrm.at[core, role, rows], nrm.at[core, role, rows], dsend.at[role, which], drecv.at[role, which],
            hid_device(OWN, True),
        )

    first = [True, True]

    def multiply(role, theirs):
        side = 1 - core if theirs else core
        if theirs:
            d_copies[role, A].wait_recv()
            d_copies[role, B].wait_recv()
        else:
            for i in range(n_weights):
                w_copies[role, i].wait()
        fresh = first[theirs]
        first[theirs] = False

        def column_tile(n, carry):
            cols = pl.ds(pl.multiple_of(n * 256, 256), 256)
            term = jnp.dot(nrm[side, role], wbuf[role, :, cols], preferred_element_type=F32)
            if fresh:
                acc[side, :, cols] = term
            else:
                acc[side, :, cols] += term
            return carry

        lax.fori_loop(0, width // 256, column_tile, 0)

    if free is not None:
        pl.semaphore_wait(free, 1)
    normalize(OWN, A)
    normalize(OWN, B)
    await_raw(ZM, A)
    send_raw(ZM, A, ZP, Z2)
    await_raw(ZP, B)
    send_raw(ZP, B, ZM, Z2)
    await_raw(XP, A)
    send_raw(XP, A, ZP, ZMX)
    send_raw(XP, A, ZM, ZPX)
    multiply(OWN, False)
    normalize(ZM, A)
    normalize(ZP, B)
    normalize(XP, A)
    multiply(OWN, True)
    await_raw(XP, B)
    send_raw(XP, B, ZP, ZMX)
    send_raw(XP, B, ZM, ZPX)
    normalize(XP, B)
    await_raw(ZM, B)
    normalize(ZM, B)
    multiply(XP, False)
    await_raw(ZP, A)
    normalize(ZP, A)
    multiply(ZM, False)
    multiply(ZP, False)
    multiply(XP, True)
    if meanwhile:
        meanwhile()
    await_raw(Z2, A)
    send_raw(Z2, A, XP, Z2X)
    await_raw(Z2, B)
    send_raw(Z2, B, XP, Z2X)
    normalize(Z2, A)
    normalize(Z2, B)
    multiply(ZM, True)
    multiply(ZP, True)
    multiply(Z2, False)
    multiply(Z2, True)
    await_raw(ZMX, A)
    normalize(ZMX, A)
    await_raw(ZPX, A)
    normalize(ZPX, A)
    await_raw(Z2X, A)
    normalize(Z2X, A)
    await_raw(ZMX, B)
    normalize(ZMX, B)
    await_raw(ZPX, B)
    normalize(ZPX, B)
    multiply(ZMX, False)
    await_raw(Z2X, B)
    normalize(Z2X, B)
    multiply(ZPX, False)
    multiply(Z2X, False)
    multiply(ZMX, True)
    multiply(ZPX, True)
    multiply(Z2X, True)
    for cp in stat_copies + list(sends.values()) + list(d_copies.values()):
        cp.wait_send()


def head_norm_phase(acc, gains, outs, qstat, qsend, qrecv, meanwhile):
    half = acc.shape[1]
    wq = outs[0].shape[1]
    for side in range(2):
        for i in range(2):
            values = acc[side, :, i * wq:(i + 1) * wq]
            qstat[0, 2 * side + i:2 * side + i + 1] = lane_sums(values * values)
    copies = []
    for flip in (False, True):
        for role in range(8):
            if role == OWN and not flip:
                continue
            there = BACK[role] + 8 * flip
            copies.append(
                remote(qstat.at[0], qstat.at[there], qsend.at[role + 8 * flip], qrecv.at[there], hid_device(role, flip))
            )
    for side in range(2):
        outs[2][pl.ds(side * half, half)] = acc[side, :, 2 * wq:3 * wq].astype(BF16)
    meanwhile()
    for cp in copies:
        cp.wait_recv()
    sums = qstat[0]
    for i in range(1, 16):
        sums = sums + qstat[i]
    scales = lax.rsqrt(rows_to_columns(sums * (1.0 / (16 * wq)), 128) + EPS)
    for side in range(2):
        for i in range(2):
            at = (2 * side + i) * 128
            by = scales[:, at:at + 1] * (SCORE_SCALE if i == 0 else 1.0)
            outs[i][pl.ds(side * half, half)] = (acc[side, :, i * wq:(i + 1) * wq] * by * gains[i][...]).astype(BF16)
    for cp in copies:
        cp.wait_send()


def attend_phase(q_ref, k_ref, v_ref, clip_ref, out_ref, qb, kb, vb, crow, best, acc, obuf,
                 xsend, xrecv, ysend, yrecv, csend, crecv, osem):
    rows = q_ref.shape[0]
    tile = rows // 2
    xh = lax.rem(lax.axis_index("seq"), 2)
    mine = pl.ds(pl.multiple_of(xh * HEAD_DIM, HEAD_DIM), HEAD_DIM)
    other = pl.ds(pl.multiple_of((1 - xh) * HEAD_DIM, HEAD_DIM), HEAD_DIM)
    low = pl.ds(0, HEAD_DIM)
    peers = [(y, f) for y in range(4) for f in (0, 1) if (y, f) != (0, 0)]
    def to(src, dst, send_sem, recv_sem, y, f):
        return pltpu.make_async_remote_copy(
            src, dst, send_sem, recv_sem, device_id=seq_device(y, f), device_id_type=MESH
        )

    def clip_copy(y, f):
        there = Y_BACK[y] * 2 + f
        return to(crow.at[0], crow.at[there], csend.at[y * 2 + f], crecv.at[there], y, f)

    x_copies = {
        "k": lambda: to(k_ref.at[:, other], kb.at[1, :, low], xsend.at[0], xrecv.at[0], 0, 1),
        "v": lambda: to(v_ref.at[:, other], vb.at[1, :, low], xsend.at[1], xrecv.at[1], 0, 1),
        "q": lambda: to(q_ref.at[:, other], qb.at[pl.ds(rows, rows), low], xsend.at[2], xrecv.at[2], 0, 1),
    }

    routes = {
        ("k", 2): (0, 2), ("k", 4): (0, 1), ("k", 3): (1, 2), ("k", 5): (1, 1), ("k", 6): (2, 2), ("k", 7): (3, 2),
        ("v", 2): (0, 2), ("v", 4): (0, 1), ("v", 3): (1, 2), ("v", 5): (1, 1), ("v", 6): (4, 1), ("v", 7): (5, 1),
    }

    def y_copy(name, to_slot):
        slot, y_role = routes[name, to_slot]
        buf, which = (kb, 0) if name == "k" else (vb, 1)
        return to(
            buf.at[slot, :, low], buf.at[to_slot, :, low],
            ysend.at[which, to_slot], yrecv.at[which, to_slot], y_role, 0,
        )

    def send_clips():
        crow[0] = clip_ref[...]
        for y, f in peers:
            clip_copy(y, f).start()

    def send_values():
        vb[0, :, 0:HEAD_DIM] = v_ref[:, mine]
        y_copy("v", 4).start()
        y_copy("v", 2).start()
        x_copies["v"]().start()

    def send_keys():
        kb[0, :, 0:HEAD_DIM] = k_ref[:, mine]
        y_copy("k", 2).start()
        y_copy("k", 4).start()
        x_copies["k"]().start()
        x_copies["q"]().start()

    def mark_keys(slot):
        kb[slot, :, HEAD_DIM:2 * HEAD_DIM] = jnp.where(clip_one_hot(crow[slot], HEAD_DIM, HEAD_DIM), 0.0, FAR).astype(BF16)

    def mark_queries(side):
        qb[pl.ds(pl.multiple_of(side * rows, rows), rows), HEAD_DIM:2 * HEAD_DIM] = (
            clip_one_hot(crow[side], HEAD_DIM, HEAD_DIM).astype(F32).astype(BF16)
        )

    def attend_pair(slot, side):
        ats = [pl.ds(pl.multiple_of(side * rows + i * tile, tile), tile) for i in range(2)]
        scores = [
            lax.dot_general(qb[at], kb[slot], (((1,), (1,)), ((), ())), preferred_element_type=F32) for at in ats
        ]
        olds = [best[at] for at in ats]
        before = [acc[at] for at in ats]
        done = []
        for i in range(2):
            old = olds[i][:, 0:1]
            fresh = jnp.maximum(old, jnp.max(scores[i], axis=1, keepdims=True))
            weights = jnp.exp2(scores[i] - fresh).astype(BF16)
            mixed = jnp.dot(weights, vb[slot], preferred_element_type=F32)
            done.append((fresh, before[i] * jnp.exp2(old - fresh) + mixed))
        for i in range(2):
            best[ats[i]] = jnp.broadcast_to(done[i][0], (tile, HEAD_DIM))
            acc[ats[i]] = done[i][1]

    def prepare():
        best[...] = jnp.full(best.shape, 3.0 * FAR, F32)
        acc[...] = jnp.zeros_like(acc)
        for y, f in peers:
            clip_copy(y, f).wait_recv()

        def mark_slot(slot, carry):
            mark_keys(slot)
            vb[slot, :, HEAD_DIM:2 * HEAD_DIM] = jnp.ones((rows, HEAD_DIM), BF16)
            return carry

        def mark_side(side, carry):
            mark_queries(side)
            return carry

        lax.fori_loop(0, 8, mark_slot, 0)
        lax.fori_loop(0, 2, mark_side, 0)

    def early(i, carry):
        @pl.when(i == 1)
        def _():
            y_copy("v", 4).wait_recv()
            y_copy("v", 6).start()
            x_copies["v"]().wait_recv()
            y_copy("v", 5).start()
            y_copy("v", 3).start()
            y_copy("k", 2).wait_recv()
            y_copy("k", 6).start()
            x_copies["k"]().wait_recv()
            y_copy("k", 3).start()
            y_copy("k", 5).start()

        @pl.when(i == 2)
        def _():
            y_copy("v", 2).wait_recv()

        @pl.when(i == 3)
        def _():
            y_copy("k", 4).wait_recv()

        @pl.when(i == 4)
        def _():
            x_copies["q"]().wait_recv()

        j = lax.rem(i, 4)
        attend_pair(j + j // 3, i // 4)
        return carry

    def finished(side):
        at = pl.ds(side * rows, rows)
        return (acc[at, 0:HEAD_DIM] / acc[at, HEAD_DIM:2 * HEAD_DIM]).astype(BF16)

    def back():
        return to(obuf, out_ref.at[:, mine], osem.at[0], osem.at[1], 0, 1)

    def late(i, carry):
        @pl.when(i == 0)
        def _():
            y_copy("k", 3).wait_recv()
            y_copy("k", 7).start()
            y_copy("v", 5).wait_recv()
            y_copy("v", 7).start()
            y_copy("k", 6).wait_recv()
            y_copy("v", 6).wait_recv()

        @pl.when(i == 2)
        def _():
            y_copy("v", 3).wait_recv()

        @pl.when(i == 4)
        def _():
            y_copy("k", 5).wait_recv()

        @pl.when(i == 6)
        def _():
            y_copy("k", 7).wait_recv()
            y_copy("v", 7).wait_recv()

        @pl.when(i == 7)
        def _():
            obuf[...] = finished(1)
            back().start()

        p = i // 2
        attend_pair(6 - 3 * p + 5 * (p // 2) + 5 * (p // 3), lax.rem(i + p // 3, 2))
        return carry

    def run():
        qb[pl.ds(0, rows), 0:HEAD_DIM] = q_ref[:, mine]
        lax.fori_loop(0, 8, early, 0)
        lax.fori_loop(0, 8, late, 0)
        out_ref[:, mine] = finished(0)
        back().wait()
        for y, f in peers:
            clip_copy(y, f).wait_send()
        for name in x_copies:
            x_copies[name]().wait_send()
        for name, slot in routes:
            y_copy(name, slot).wait_send()

    return send_clips, prepare, send_values, send_keys, run


def scatter_phase(a_ref, w_copies, own, hot_ref, gate_ref, wbuf, terms, got, land, gate_buf,
                  dsend, drecv, nsend, nrecv):
    depth, full = wbuf.shape[1], wbuf.shape[2]
    half = got.shape[1]
    part = terms.at[0]
    quarter = half // 2
    core = hid_place()[2]
    d_copies = {}
    arrived = {}

    def multiply(role):
        w_copies[role].wait()

        def row_half(i, carry):
            side = lax.rem(core + i, 2)
            rows = pl.ds(pl.multiple_of(side * half, half), half)
            terms[i, role] = jnp.dot(a_ref[rows], wbuf[role], preferred_element_type=F32).astype(BF16)
            return carry

        lax.fori_loop(0, 2, row_half, 0)
        d_copies[role] = remote(
            terms.at[1, role], got.at[role], dsend.at[role], drecv.at[role], hid_device(OWN, True)
        )

    def send(role, which, to_role, slot):
        rows = pl.ds(which * quarter, quarter)
        arrived[slot, which] = remote(
            part.at[role, rows], land.at[slot, rows], nsend.at[slot, which], nrecv.at[slot, which],
            hid_device(to_role, False),
        )

    def fold(role, which, slots=(), last=False):
        rows = pl.ds(which * quarter, quarter)
        for slot in slots:
            arrived[slot, which].wait_recv()

        def lane_tile(n, carry):
            here = pl.ds(pl.multiple_of(n * 128, 128), 128)
            value = part[role, rows, here].astype(F32) + got[role, rows, here].astype(F32)
            for slot in slots:
                value = value + land[slot, rows, here].astype(F32)
            if last:
                own[rows, here] = (own[rows, here].astype(F32) + gate_buf[rows, here] * value).astype(BF16)
            else:
                part[role, rows, here] = value.astype(BF16)
            return carry

        lax.fori_loop(0, full // 128, lane_tile, 0)

    multiply(Z2X)
    multiply(ZPX)
    multiply(ZMX)
    d_copies[Z2X].wait_recv()
    fold(Z2X, A)
    send(Z2X, A, XP, 0)
    fold(Z2X, B)
    send(Z2X, B, XP, 0)
    d_copies[ZPX].wait_recv()
    fold(ZPX, A)
    send(ZPX, A, ZP, 1)
    d_copies[ZMX].wait_recv()
    fold(ZMX, A)
    send(ZMX, A, ZM, 2)
    fold(ZPX, B)
    send(ZPX, B, ZP, 1)
    fold(ZMX, B)
    send(ZMX, B, ZM, 2)
    multiply(Z2)
    multiply(ZP)
    multiply(ZM)
    d_copies[Z2].wait_recv()
    fold(Z2, A, (0,))
    send(Z2, A, ZP, 3)
    multiply(XP)
    d_copies[ZP].wait_recv()
    fold(ZP, B)
    d_copies[ZM].wait_recv()
    fold(ZM, A)
    d_copies[XP].wait_recv()
    fold(XP, A, (1, 2))
    send(XP, A, XP, 7)
    fold(Z2, B, (0,))
    send(Z2, B, ZM, 4)
    send(ZP, B, ZP, 5)
    send(ZM, A, ZM, 6)
    multiply(OWN)
    fold(XP, B, (1, 2))
    send(XP, B, XP, 7)
    fold(ZP, A, (3,))
    send(ZP, A, ZP, 5)
    fold(ZM, B, (4,))
    send(ZM, B, ZM, 6)
    hot_rows = hot_ref[pl.ds(pl.multiple_of(core * half, half), half)]
    gate_buf[...] = jnp.dot(hot_rows, pieces(gate_ref[...], 3), preferred_element_type=F32)
    d_copies[OWN].wait_recv()
    fold(OWN, A, (7, 6, 5), True)
    fold(OWN, B, (7, 5, 6), True)
    for cp in list(arrived.values()) + list(d_copies.values()):
        cp.wait_send()


def unpair_rows(own, result, theirs, fsem):
    half, full = own.shape
    part = full // 2
    core = hid_place()[2]
    rows = pl.ds(core * half, half)
    values = own[...].astype(F32)
    turned = pltpu.roll(values, part, 1)
    theirs[...] = jnp.where(core == 0, turned, values)[:, 0:part].astype(BF16)
    back = remote(theirs, result.at[rows], fsem.at[0], fsem.at[1], hid_device(OWN, True))
    result[rows] = jnp.where(core == 0, values, turned)[:, 0:part].astype(BF16)
    back.wait()


GATHER_SEMS = [(8,), (8,), (8, 2), (8, 2), (8, 2), (8, 2)]
ATTEND_SEMS = [(3,), (3,), (2, 8), (2, 8), (8,), (8,), (2,)]
SCATTER_SEMS = [(8,), (8,), (8, 2), (8, 2)]


def sems(shapes):
    return [pltpu.SemaphoreType.DMA(s) for s in shapes]


def gather_scratch(half, full, width):
    return [
        pltpu.VMEM((8, half, full), BF16),
        pltpu.VMEM((2, 8, half, full), BF16),
        pltpu.VMEM((8, 2, half), F32),
        pltpu.VMEM((2, half, 128), F32),
        pltpu.VMEM((8, full, width), BF16),
        pltpu.VMEM((2, half, width), F32),
    ]


def attend_scratch(rows):
    return [
        pltpu.VMEM((2 * rows, 2 * HEAD_DIM), BF16),
        pltpu.VMEM((8, rows, 2 * HEAD_DIM), BF16),
        pltpu.VMEM((8, rows, 2 * HEAD_DIM), BF16),
        pltpu.VMEM((8, 1, rows), F32),
        pltpu.VMEM((2 * rows, HEAD_DIM), F32),
        pltpu.VMEM((2 * rows, 2 * HEAD_DIM), F32),
        pltpu.VMEM((rows, HEAD_DIM), BF16),
    ]


def scatter_scratch(half, full):
    return [pltpu.VMEM((8, half, full), BF16), pltpu.VMEM((8, half, full), BF16), pltpu.VMEM((half, full), F32)]


def block_kernel(tokens, clip_ids, clip_step, table, w_query, w_key, w_value, q_gain, k_gain, w_out, w_up, w_down, out_ref,
                 x_turned, clip_ref, mods, gates, x, pair, hot, q, k, v, attended, hidden, qstat, w_first, w_mix,
                 w_last, acc, *refs):
    (x_sem, t_sem, p_sem, w_sem, up_sem, mix_sem, last_sem, qs_sem, qr_sem, free), refs = refs[:10], refs[10:]
    gather_bufs, refs = refs[:4], refs[4:]
    attend_bufs, refs = refs[:7], refs[7:]
    raw = gather_bufs[0]
    scatter_bufs, refs = (gather_bufs[1],) + refs[:3], refs[3:]
    gather_sems, attend_sems, scatter_sems = refs[:6], refs[6:13], refs[13:]
    half = acc.shape[1]
    width = w_query.shape[1]
    wide = w_up.shape[1]

    part, full = x.shape[1], w_last.shape[2]
    x_copy = pltpu.make_async_copy(tokens, x_turned, x_sem.at[0])
    x_copy.start()
    t_copies = [
        pltpu.make_async_copy(table.at[c], mods.at[i], t_sem.at[i]) for i, c in enumerate((0, 1, 3, 4))
    ] + [
        pltpu.make_async_copy(
            table.at[c, :, pl.ds(pl.multiple_of(chip_of(OWN) * full, 128), full)], gates.at[i], t_sem.at[4 + i]
        )
        for i, c in enumerate((2, 5))
    ]
    for cp in t_copies:
        cp.start()
    first = load_columns_of_rows((w_query, w_key, w_value), w_first, w_sem, (width,) * 3)
    clip_ref[...] = clip_ids[...].astype(F32).reshape(clip_ref.shape)
    clip_hot = clip_one_hot(clip_ref[...], 8, 8).astype(F32).astype(BF16)
    steps = lax.dot_general(
        clip_step[...].astype(F32).astype(BF16), jnp.ones((1, hot.shape[1]), BF16), (((0,), (0,)), ((), ())),
        preferred_element_type=F32,
    )
    lane = lax.rem(lax.broadcasted_iota(jnp.int32, steps.shape, 1), hot.shape[1] // 3).astype(F32)
    step_hot = (steps == lane).astype(F32).astype(BF16)
    hot[...] = jnp.dot(clip_hot, step_hot, preferred_element_type=F32).astype(BF16)
    x_copy.wait()
    x[...] = lax.dot_general(
        x_turned[...], identity(part), (((0,), (0,)), ((), ())), preferred_element_type=F32
    ).astype(BF16)
    greet(True, True, True)
    send_clips, prepare, send_values, send_keys, attend = attend_phase(
        q, k, v, clip_ref, attended, *attend_bufs, *attend_sems
    )
    pair_rows(x, raw, pair, p_sem)
    send_clips()
    for cp in t_copies:
        cp.wait()
    gather_phase(hot, mods, 1, first, 3, 3 * width, *gather_bufs, w_first, acc, *gather_sems, meanwhile=prepare)
    head_norm_phase(acc, (q_gain, k_gain), (q, k, v), qstat, qs_sem, qr_sem, send_values)
    send_keys()
    mix = load_blocks_of_columns(w_out, w_mix, mix_sem)
    up = load_columns_of_rows((w_up,), w_first, up_sem, (wide,))
    last = load_blocks_of_columns(w_down, w_last, last_sem)
    attend()
    scatter_phase(attended, mix, raw.at[OWN], hot, gates.at[0], w_mix, *scatter_bufs, *scatter_sems)
    pl.semaphore_signal(free, inc=1, device_id=hid_device(OWN, True), device_id_type=MESH)
    gather_phase(hot, mods, 3, up, 1, wide, *gather_bufs, w_first, acc, *gather_sems, free=free)
    for side in range(2):
        hidden[pl.ds(side * half, half)] = jax.nn.gelu(acc[side, :, 0:wide], approximate=True).astype(BF16)
    scatter_phase(hidden, last, raw.at[OWN], hot, gates.at[1], w_last, *scatter_bufs, *scatter_sems)
    unpair_rows(raw.at[OWN], x, pair, p_sem)
    out_ref[...] = lax.dot_general(
        identity(part), x[...], (((1,), (1,)), ((), ())), preferred_element_type=F32
    ).astype(BF16)


def block(tokens_turned, clip_id, clip_step, table, w_query, w_key, w_value, q_gain, k_gain, w_out, w_up, w_down):
    part, rows = tokens_turned.shape
    steps = table.shape[1]
    half, full = rows // 2, 2 * part
    width, wide = w_query.shape[1], w_up.shape[1]
    gather = gather_scratch(half, full, 3 * width)
    scratch = [
        pltpu.VMEM((part, rows), BF16),
        pltpu.VMEM((1, rows), F32),
        pltpu.VMEM((4, steps, table.shape[2]), F32),
        pltpu.VMEM((2, steps, full), F32),
        pltpu.VMEM((rows, part), BF16),
        pltpu.VMEM((half, part), BF16),
        pltpu.VMEM((rows, 3 * steps), BF16),
        pltpu.VMEM((rows, width), BF16),
        pltpu.VMEM((rows, width), BF16),
        pltpu.VMEM((rows, width), BF16),
        pltpu.VMEM((rows, width), BF16),
        pltpu.VMEM((rows, wide), BF16),
        pltpu.VMEM((16, 4, half), F32),
        gather[4],
        pltpu.VMEM((8, width, full), BF16),
        pltpu.VMEM((8, wide, full), BF16),
        gather[5],
    ]
    scratch += sems([(1,), (6,), (2,), (8, 3), (8, 1), (8,), (8,), (16,), (16,)])
    scratch += [pltpu.SemaphoreType.REGULAR]
    scratch += gather[:4] + attend_scratch(rows) + scatter_scratch(half, full)
    scratch += sems(GATHER_SEMS + ATTEND_SEMS + SCATTER_SEMS)
    return pl.pallas_call(
        block_kernel,
        out_shape=jax.ShapeDtypeStruct((part, rows), BF16),
        in_specs=[ANYSPEC, VSPEC, VSPEC, ANYSPEC, ANYSPEC, ANYSPEC, ANYSPEC, VSPEC, VSPEC, ANYSPEC, ANYSPEC, ANYSPEC],
        out_specs=VSPEC,
        scratch_shapes=scratch,
        compiler_params=pltpu.CompilerParams(collective_id=1, has_side_effects=True, vmem_limit_bytes=60 << 20),
        name="block",
    )(tokens_turned, clip_id, clip_step, table, w_query, w_key, w_value, q_gain, k_gain, w_out, w_up, w_down)


def shards(tokens, clip_id, clip_step, mod_table, w_query, w_key, w_value, q_gain, k_gain, w_out, w_up, w_down):
    return block(
        tokens.T, clip_id, clip_step[None, :], mod_table.transpose(1, 0, 2), w_query, w_key, w_value,
        q_gain[None, :], k_gain[None, :], w_out, w_up, w_down,
    ).T


def solution(mesh):
    placed = (
        P("seq", "hid"), P("seq"), P(), P(), P(None, "hid"), P(None, "hid"), P(None, "hid"), P("hid"), P("hid"),
        P("hid", None), P(None, "hid"), P("hid", None),
    )
    return jax.shard_map(shards, mesh=mesh, in_specs=placed, out_specs=P("seq", "hid"), check_vma=False)
```

profile of v0, /device:TPU:1, one launch (start us, length us, event | category | flops | bytes accessed | tf_op | source)
XLA Modules:
  0.0 189.2 jit_solution(16178350655880698093)
XLA Ops:
  0.0 187.4 %block.1 = bf16[320,640]{1,0:T(8,128)(2,1)} custom-call(bf16[320,640]{1,0:T(8,128)(2,1)} %bitcast.8, s32[640]{0:T(1024)} %clip_ids.1, s32[1,8]{1,0:T(1,128)} %bitcast.11, f32[6,32,5120]{2,1,0:T(8,128)} %bitcast.6, bf16[5120,256]{1,0:T(8,128)(2,1)} %w_query.1, bf16[5120,256]{1,0:T(8,128)(2,1)} %w_key.1, bf16[5120,256]{1,0:T(8,128)(2,1)} %w_value.1, ...), custom_call_target="tpu_custom_call" | custom-call | tf_op jit(solution)/shard_map/block/pallas_call | solution.py:773
  187.4 1.8 copy.14
where the time goes:
time: 189 us
  Pallas kernels  187 us (99%)
    pallas_call x1, Pallas kernels, block(): pl.pallas_call(block_kernel, out_shape=jax.ShapeDtypeStruct((part, rows),...  187 us

commit v1 on v0

--- a/solution.py
+++ b/solution.py
@@ -94,7 +94,7 @@
         peers += [seq_device(y, f) for y in range(4) for f in (False, True) if (y, f) != (0, False)]
     for peer in peers:
         pl.semaphore_signal(barrier, inc=1, device_id=peer, device_id_type=MESH)
-    pl.semaphore_wait(barrier, len(peers))
+    return lambda: pl.semaphore_wait(barrier, len(peers))
 
 
 def remote(src, dst, send_sem, recv_sem, device):
@@ -260,6 +260,8 @@
     normalize(ZP, B)
     normalize(XP, A)
     multiply(OWN, True)
+    if meanwhile:
+        meanwhile()
     await_raw(XP, B)
     send_raw(XP, B, ZP, ZMX)
     send_raw(XP, B, ZM, ZPX)
@@ -272,8 +274,6 @@
     multiply(ZM, False)
     multiply(ZP, False)
     multiply(XP, True)
-    if meanwhile:
-        meanwhile()
     await_raw(Z2, A)
     send_raw(Z2, A, XP, Z2X)
     await_raw(Z2, B)
@@ -393,7 +393,6 @@
         y_copy("k", 2).start()
         y_copy("k", 4).start()
         x_copies["k"]().start()
-        x_copies["q"]().start()
 
     def mark_keys(slot):
         kb[slot, :, HEAD_DIM:2 * HEAD_DIM] = jnp.where(clip_one_hot(crow[slot], HEAD_DIM, HEAD_DIM), 0.0, FAR).astype(BF16)
@@ -442,15 +441,16 @@
     def early(i, carry):
         @pl.when(i == 1)
         def _():
-            y_copy("v", 4).wait_recv()
-            y_copy("v", 6).start()
             x_copies["v"]().wait_recv()
             y_copy("v", 5).start()
-            y_copy("v", 3).start()
-            y_copy("k", 2).wait_recv()
-            y_copy("k", 6).start()
             x_copies["k"]().wait_recv()
             y_copy("k", 3).start()
+            x_copies["q"]().start()
+            y_copy("k", 2).wait_recv()
+            y_copy("v", 4).wait_recv()
+            y_copy("k", 6).start()
+            y_copy("v", 6).start()
+            y_copy("v", 3).start()
             y_copy("k", 5).start()
 
         @pl.when(i == 2)
@@ -690,6 +690,7 @@
     part, full = x.shape[1], w_last.shape[2]
     x_copy = pltpu.make_async_copy(tokens, x_turned, x_sem.at[0])
     x_copy.start()
+    everyone_here = greet(True, True, True)
     t_copies = [
         pltpu.make_async_copy(table.at[c], mods.at[i], t_sem.at[i]) for i, c in enumerate((0, 1, 3, 4))
     ] + [
@@ -714,7 +715,7 @@
     x[...] = lax.dot_general(
         x_turned[...], identity(part), (((0,), (0,)), ((), ())), preferred_element_type=F32
     ).astype(BF16)
-    greet(True, True, True)
+    everyone_here()
     send_clips, prepare, send_values, send_keys, attend = attend_phase(
         q, k, v, clip_ref, attended, *attend_bufs, *attend_sems
     )
@@ -722,13 +723,13 @@
     send_clips()
     for cp in t_copies:
         cp.wait()
+    mix = load_blocks_of_columns(w_out, w_mix, mix_sem)
+    last = load_blocks_of_columns(w_down, w_last, last_sem)
     gather_phase(hot, mods, 1, first, 3, 3 * width, *gather_bufs, w_first, acc, *gather_sems, meanwhile=prepare)
     head_norm_phase(acc, (q_gain, k_gain), (q, k, v), qstat, qs_sem, qr_sem, send_values)
     send_keys()
-    mix = load_blocks_of_columns(w_out, w_mix, mix_sem)
+    attend()
     up = load_columns_of_rows((w_up,), w_first, up_sem, (wide,))
-    last = load_blocks_of_columns(w_down, w_last, last_sem)
-    attend()
     scatter_phase(attended, mix, raw.at[OWN], hot, gates.at[0], w_mix, *scatter_bufs, *scatter_sems)
     pl.semaphore_signal(free, inc=1, device_id=hid_device(OWN, True), device_id_type=MESH)
     gather_phase(hot, mods, 3, up, 1, wide, *gather_bufs, w_first, acc, *gather_sems, free=free)

time: 189 us -> 185 us (0.979)
  Pallas kernels: 187 us -> 183 us
    pallas_call x1, Pallas kernels: 187 us -> 183 us  [block(): pl.pallas_call(block_kernel, out_shape=jax.ShapeDtypeStruct((part, rows),...]
where the time goes in v1:
time: 185 us; the launch traced here: 184 us
  Pallas kernels  183 us (99%)
    pallas_call x1, Pallas kernels, block(): pl.pallas_call(block_kernel, out_shape=jax.ShapeDtypeStruct((part, rows),...  183 us

profile of v1, /device:TPU:1, one launch (start us, length us, event | category | flops | bytes accessed | tf_op | source)
XLA Modules:
  0.0 184.4 jit_solution(15464948687454180551)
XLA Ops:
  0.0 182.6 %block.1 = bf16[320,640]{1,0:T(8,128)(2,1)} custom-call(bf16[320,640]{1,0:T(8,128)(2,1)} %bitcast.8, s32[640]{0:T(1024)} %clip_ids.1, s32[1,8]{1,0:T(1,128)} %bitcast.11, f32[6,32,5120]{2,1,0:T(8,128)} %bitcast.6, bf16[5120,256]{1,0:T(8,128)(2,1)} %w_query.1, bf16[5120,256]{1,0:T(8,128)(2,1)} %w_key.1, bf16[5120,256]{1,0:T(8,128)(2,1)} %w_value.1, ...), custom_call_target="tpu_custom_call" | custom-call | tf_op jit(solution)/shard_map/block/pallas_call | solution.py:774
  182.6 1.8 copy.14

commit v2 on v1

--- a/solution.py
+++ b/solution.py
@@ -543,10 +543,11 @@
             terms[i, role] = jnp.dot(a_ref[rows], wbuf[role], preferred_element_type=F32).astype(BF16)
             return carry
 
-        lax.fori_loop(0, 2, row_half, 0)
+        row_half(1, 0)
         d_copies[role] = remote(
             terms.at[1, role], got.at[role], dsend.at[role], drecv.at[role], hid_device(OWN, True)
         )
+        row_half(0, 0)
 
     def send(role, which, to_role, slot):
         rows = pl.ds(which * quarter, quarter)
@@ -575,12 +576,12 @@
 
     multiply(Z2X)
     multiply(ZPX)
-    multiply(ZMX)
     d_copies[Z2X].wait_recv()
     fold(Z2X, A)
     send(Z2X, A, XP, 0)
     fold(Z2X, B)
     send(Z2X, B, XP, 0)
+    multiply(ZMX)
     d_copies[ZPX].wait_recv()
     fold(ZPX, A)
     send(ZPX, A, ZP, 1)

time: 185 us -> 184 us (level)
  no operation moved by 1% of the time
where the time goes in v2:
time: 184 us
  Pallas kernels  182 us (99%)
    pallas_call x1, Pallas kernels, block(): pl.pallas_call(block_kernel, out_shape=jax.ShapeDtypeStruct((part, rows),...  182 us

profile of v2, /device:TPU:1, one launch (start us, length us, event | category | flops | bytes accessed | tf_op | source)
XLA Modules:
  0.0 184.1 jit_solution(13547085490143760323)
XLA Ops:
  0.0 182.3 %block.1 = bf16[320,640]{1,0:T(8,128)(2,1)} custom-call(bf16[320,640]{1,0:T(8,128)(2,1)} %bitcast.8, s32[640]{0:T(1024)} %clip_ids.1, s32[1,8]{1,0:T(1,128)} %bitcast.11, f32[6,32,5120]{2,1,0:T(8,128)} %bitcast.6, bf16[5120,256]{1,0:T(8,128)(2,1)} %w_query.1, bf16[5120,256]{1,0:T(8,128)(2,1)} %w_key.1, bf16[5120,256]{1,0:T(8,128)(2,1)} %w_value.1, ...), custom_call_target="tpu_custom_call" | custom-call | tf_op jit(solution)/shard_map/block/pallas_call | solution.py:775
  182.3 1.8 copy.14
